TPU v7x, 256 devices: a whole 4x4x8 slice. The times are simulated.
256 devices in a mesh: band: 8 (over y_hi, x), item: 32 (over y_lo, z, core).
Axes of the slice: x: 4, y: 4 (y_hi: 2, y_lo: 2; y = y_hi * 2 + y_lo), z: 8, core: 2. Of those that a mesh axis runs over, the one named last changes fastest.
Arguments:
- ratings: bfloat16 [49152, 16384], P('band', 'item'), may hold values from -6 to 6
- rating_mask: int32 [384, 16384], P('band', 'item'), may hold values 0 or 1
- attributes: bfloat16 [24576, 16384], P('band', 'item'), may hold values from -6 to 6
- attribute_mask: int32 [192, 16384], P('band', 'item'), may hold values 0 or 1
- user_factors: bfloat16 [49152, 256], P('band', 'item'), as said below
- tag_factors: bfloat16 [24576, 256], P('band', 'item'), as said below
Outputs:
- item_factors: float32 [16384, 256], P('item')
Inputs may be any that keep to these rules, and one draw needn't show every extreme that they name: `user_factors`: user factors of order one over the square root of 49152. `tag_factors`: tag factors of order one over the square root of 24576.
All inputs are finite; a program needn't handle non-finite values. No bound on the sum of `rating_mask` or of `attribute_mask` on one device may be relied on, other than what follows from the above.
Results may differ from a plain program's by a relative error of at most 0.0003.
Values may be sent and summed in bfloat16 or wider, within the bound.
No kernel may reach another device: no remote copies, remote signals or barrier semaphores. Data moves between devices by JAX's collectives and lax.ppermute only.
A program may use at most 64 MiB of HBM per device.

v0:
```python
import jax
import jax.numpy as jnp
from jax import lax
from jax.sharding import PartitionSpec as P

LAMBDA = 0.5
REG = 0.1


def apply_mask(values, mask):
    rows, cols = values.shape
    blocks = mask.shape[0]
    shaped = values.reshape(blocks, rows // blocks, cols) * mask.astype(values.dtype)[:, None, :]
    return shaped.reshape(rows, cols)


def inner(left, right):
    return lax.dot_general(
        left, right, (((0,), (0,)), ((), ())), preferred_element_type=jnp.float32
    )


def solve_rows(factor, rhs):
    half = lax.linalg.triangular_solve(factor, rhs, left_side=False, lower=True, transpose_a=True)
    return lax.linalg.triangular_solve(factor, half, left_side=False, lower=True, transpose_a=False)


def band_gram(partial_gram):
    return lax.psum(partial_gram, "band")


def finish_gram(summed_gram, rank):
    return jnp.linalg.cholesky(summed_gram + REG * jnp.eye(rank, dtype=jnp.float32))


def body(ratings, rating_mask, attributes, attribute_mask, user_factors, tag_factors):
    users = lax.all_gather(user_factors, "item", axis=1, tiled=True)
    tags = lax.all_gather(tag_factors, "item", axis=1, tiled=True)
    rank = users.shape[1]
    partial_gram = inner(users, users) + LAMBDA * inner(tags, tags)
    masked_ratings = apply_mask(ratings, rating_mask)
    masked_attributes = apply_mask(attributes, attribute_mask)
    local_rhs = inner(masked_ratings, users) + LAMBDA * inner(masked_attributes, tags)
    summed_gram = band_gram(partial_gram)
    summed_rhs = lax.psum(local_rhs, "band")
    factor = finish_gram(summed_gram, rank)
    return solve_rows(factor, summed_rhs)


def solution(mesh):
    in_specs = (
        P("band", "item"),
        P("band", "item"),
        P("band", "item"),
        P("band", "item"),
        P("band", "item"),
        P("band", "item"),
    )
    out_specs = P("item", None)
    return jax.shard_map(body, mesh=mesh, in_specs=in_specs, out_specs=out_specs, check_vma=False)
```

profile of v0, /device:TPU:32, one launch (start us, length us, event | category | flops | bytes accessed | tf_op | source)
XLA Modules:
  0.0 317.1 jit_solution(6339761031712931756)
XLA Ops:
  6.5 0.0 all-gather.5.cloned.1.call-start
  6.5 0.7 all-gather.5.cloned.1.call-update
  7.3 0.0 all-gather.3.cloned.1.call-start
  7.3 0.7 all-gather.3.cloned.1.call-update
  8.0 0.0 all-reduce.4.cloned.1.call-start
  8.1 0.8 convert_element_type.8
  8.9 0.9 convert_element_type.7
  9.8 0.0 copy-start
  9.8 2.3 bitcast_multiply_fusion.1
  12.0 1.5 copy-done
  13.5 3.1 bitcast_multiply_fusion
  16.6 58.8 %all-gather.5.cloned.1.call-done = bf16[3072,256]{0,1:T(8,128)(2,1)} async-done(((bf16[3072,8]{0,1:T(8,128)(2,1)}), bf16[3072,256]{0,1:T(8,128)(2,1)}) %all-gather.5.cloned.1.call-update) | async-done | bytes 1572880 | tf_op jit(solution)/shard_map/all_gather | solution.py:38
  75.4 3.2 %convolution_multiply_fusion = f32[512,256]{1,0:T(8,128)} fusion(bf16[3072,512]{1,0:T(8,128)(2,1)S(1)} %bitcast_multiply_fusion.1, bf16[3072,256]{0,1:T(8,128)(2,1)} %all-gather.5.cloned.1.call-done), kind=kOutput, calls=%fused_computation.4 | convolution fusion | flops 805437440 | bytes 5242880 | tf_op jit(solution)/shard_map/dot_general | solution.py:18
  78.6 0.0 copy-start.2
  78.6 64.3 %all-gather.3.cloned.1.call-done = bf16[6144,256]{0,1:T(8,128)(2,1)} async-done(((bf16[6144,8]{0,1:T(8,128)(2,1)}), bf16[6144,256]{0,1:T(8,128)(2,1)}) %all-gather.3.cloned.1.call-update) | async-done | bytes 3145744 | tf_op jit(solution)/shard_map/all_gather | solution.py:37
  142.9 0.0 copy-start.1
  142.9 4.0 %fusion.13 = f32[256,256]{1,0:T(8,128)S(1)} fusion(bf16[6144,256]{0,1:T(8,128)(2,1)} %all-gather.3.cloned.1.call-done), kind=kOutput, calls=%fused_computation.41 | convolution fusion | flops 805306368 | bytes 3407872 | tf_op jit(solution)/shard_map/dot_general | solution.py:18
  146.9 0.0 copy-done.2
  146.9 0.0 copy-start.4
  146.9 1.3 fusion
  148.2 0.0 copy-done.1
  148.2 0.0 copy-done.4
  148.2 4.5 %convolution_add_fusion = f32[512,256]{1,0:T(8,128)} fusion(f32[512,256]{1,0:T(8,128)S(1)} %copy-done.4, bf16[6144,512]{1,0:T(8,128)(2,1)S(1)} %copy-done.1, bf16[6144,256]{0,1:T(8,128)(2,1)} %all-gather.3.cloned.1.call-done), kind=kOutput, calls=%fused_computation.5 | convolution fusion | flops 1610743808 | bytes 10485760 | tf_op jit(solution)/shard_map/dot_general | solution.py:18
  152.8 0.0 all-reduce.4.cloned.1.call-update
  152.8 92.3 %all-reduce.4.cloned.1.call-done = (f32[512,256]{1,0:T(8,128)}, f32[256,256]{1,0:T(8,128)}) async-done(((f32[512,256]{1,0:T(8,128)}, f32[256,256]{1,0:T(8,128)}), (f32[512,256]{1,0:T(8,128)}, f32[256,256]{1,0:T(8,128)})) %all-reduce.4.cloned.1.call-update) | async-done | bytes 786448 | tf_op jit(solution)/shard_map/psum | solution.py:45
  245.1 0.0 copy-start.3
  245.1 1.0 select_add_fusion
  246.2 0.1 copy.7
  246.3 1.0 fusion.3
  247.3 11.7 %cholesky.49 = f32[128,128]{1,0:T(8,128)S(1)} custom-call(f32[128,128]{1,0:T(8,128)S(1)} %cholesky.115), custom_call_target="Cholesky" | custom-call | tf_op jit(solution)/shard_map/jit(cholesky)/cholesky | solution.py:33
  259.1 9.8 %custom-call.16 = f32[1,128,128]{1,2,0:T(8,128)S(1)} custom-call(f32[1,128,128]{2,1,0:T(8,128)S(1)} %get-tuple-element.28), custom_call_target="InvertDiagBlocksLowerTriangular" | custom-call | tf_op jit(solution)/shard_map/jit(cholesky)/cholesky | solution.py:33
  268.9 0.2 constant_dynamic-update-slice_fusion.1
  269.1 0.3 convolution_subtract_fusion.2
  269.4 11.9 %cholesky.103 = f32[128,128]{1,0:T(8,128)S(1)} custom-call(f32[128,128]{1,0:T(8,128)S(1)} %convolution_subtract_fusion.2), custom_call_target="Cholesky" | custom-call | tf_op jit(solution)/shard_map/jit(cholesky)/cholesky | solution.py:33
  281.3 0.7 compare_reduce_fusion
  283.3 0.1 triangular_solve.70
  283.3 3.9 %while.1 = (s32[]{:T(128)}, f32[256,256]{1,0:T(8,128)S(1)}, s32[2,2]{1,0:T(2,128)S(1)}, f32[2,128,128]{2,1,0:T(8,128)S(1)}, s32[]{:T(128)}) while((s32[]{:T(128)}, f32[256,256]{1,0:T(8,128)S(1)}, s32[2,2]{1,0:T(2,128)S(1)}, f32[2,128,128]{2,1,0:T(8,128)S(1)}, s32[]{:T(128)}) %tuple.23), condition=%wide.while_cond, body=%wide.while_body.sunk | while | flops 2 | bytes 131189 | solution.py:24
  283.4 0.6 fusion.30
  283.9 1.4 bitcast_dynamic-update-slice_fusion.2
  285.3 0.6 fusion.30
  285.9 1.4 bitcast_dynamic-update-slice_fusion.2
  287.3 19.7 %custom-call.17 = f32[2,128,128]{1,2,0:T(8,128)S(1)} custom-call(f32[2,128,128]{2,1,0:T(8,128)S(1)} %get-tuple-element.12), custom_call_target="InvertDiagBlocksLowerTriangular" | custom-call | tf_op jit(solution)/shard_map/triangular_solve | solution.py:24
  307.0 0.0 copy-done.3
  307.0 0.4 fusion.1
  307.4 0.4 convolution_subtract_fusion.1
  307.7 0.4 fusion.9
  308.1 0.4 fusion.8
  308.5 0.6 convolution_subtract_fusion
  309.1 0.4 fusion.7
  309.6 1.0 copy.8
  (10 shorter events, 0.2 us)
Async XLA Ops:
  6.5 68.9 %all-gather.5.cloned.1.call-start = ((), (), s32[]{:S(2)}) async-start(), calls=%async_computation.1 | async-start | bytes 1622016 | tf_op jit(solution)/shard_map/all_gather | solution.py:38
  7.3 135.6 %all-gather.3.cloned.1.call-start = ((), (), s32[]{:S(2)}) async-start(), calls=%async_computation | async-start | bytes 3244032 | tf_op jit(solution)/shard_map/all_gather | solution.py:37
  8.0 237.1 %all-reduce.4.cloned.1.call-start = ((), (), s32[]{:S(2)}) async-start(), calls=%async_computation.2 | async-start | bytes 1572864 | tf_op jit(solution)/shard_map/psum | solution.py:45
  9.8 3.7 %copy-start = (bf16[6144,512]{1,0:T(8,128)(2,1)S(1)}, bf16[6144,512]{1,0:T(8,128)(2,1)}, u32[]{:S(2)}) copy-start(bf16[6144,512]{1,0:T(8,128)(2,1)} %param.6) | copy-start | bytes 18874372
  78.6 68.3 %copy-start.2 = (bf16[3072,256]{0,1:T(8,128)(2,1)S(1)}, bf16[3072,256]{0,1:T(8,128)(2,1)}, u32[]{:S(2)}) copy-start(bf16[3072,256]{0,1:T(8,128)(2,1)} %all-gather.5.cloned.1.call-done) | copy-start | bytes 4718596
  142.9 5.3 %copy-start.1 = (bf16[6144,512]{1,0:T(8,128)(2,1)S(1)}, bf16[6144,512]{1,0:T(8,128)(2,1)}, u32[]{:S(2)}) copy-start(bf16[6144,512]{1,0:T(8,128)(2,1)} %bitcast_multiply_fusion) | copy-start | bytes 18874372
  146.9 1.3 copy-start.4
  245.1 61.8 %copy-start.3 = (f32[512,256]{1,0:T(8,128)S(1)}, f32[512,256]{1,0:T(8,128)}, u32[]{:S(2)}) copy-start(f32[512,256]{1,0:T(8,128)} %get-tuple-element.21) | copy-start | bytes 1572868
Sparse Core Ops, SparseCore 0:
  9.2 66.1 all-gather.4
  77.3 65.5 all-gather.2
  152.9 92.1 all-reduce.3
where the time goes:
time: 317 us
  waiting for transfers between devices  217 us (68%)
  other arithmetic  63 us (20%)
  matrix products  16 us (5%)
  between operations  14.6 us (5%)
  local copies, waits for them, and re-layouts  6.6 us (2%)
    psum x1, waiting for transfers between devices, body(): summed_rhs = lax.psum(local_rhs, 'band')  92.3 us
    all_gather x1, waiting for transfers between devices, body(): users = lax.all_gather(user_factors, 'item', axis=1, tiled=True)  64.3 us
    all_gather x1, waiting for transfers between devices, body(): tags = lax.all_gather(tag_factors, 'item', axis=1, tiled=True)  58.8 us
    another operation x6, other arithmetic, finish_gram(): jnp.linalg.cholesky(summed_gram + REG * jnp.eye(rank, dtype=jnp.float32))  34.1 us
    another operation x3, other arithmetic, solve_rows(): lax.linalg.triangular_solve(factor, rhs, left_side=False, lower=True, tra...  19.7 us
    dot_general x4, matrix products, inner(): lax.dot_general(left, right, (((0,), (0,)), ((), ())), preferred_element_...  13 us
  transfers between devices with their start and end apart: 3, of which 3 were waited for; matrix products, arithmetic and copies ran while one was open for 3% of the time, Pallas kernels for 0%

commit v1 on v0

--- a/solution.py
+++ b/solution.py
@@ -34,7 +34,9 @@
 
 
 def body(ratings, rating_mask, attributes, attribute_mask, user_factors, tag_factors):
-    users = lax.all_gather(user_factors, "item", axis=1, tiled=True)
+    users = jnp.concatenate(
+        lax.all_to_all(jnp.stack([user_factors] * lax.axis_size("item")), "item", 0, 0), axis=1
+    )
     tags = lax.all_gather(tag_factors, "item", axis=1, tiled=True)
     rank = users.shape[1]
     partial_gram = inner(users, users) + LAMBDA * inner(tags, tags)

time: 317 us -> 279 us (0.88)
  waiting for transfers between devices: 217 us -> 166 us
  starting transfers between devices: 0.08 us -> 10.1 us
  local copies, waits for them, and re-layouts: 6.6 us -> 10.1 us
    all_gather x1 -> x0, waiting for transfers between devices: 64.3 us -> none  [body(): users = lax.all_gather(user_factors, 'item', axis=1, tiled=True)]
    all_gather x1, waiting for transfers between devices: 58.8 us -> 72.7 us  [body(): tags = lax.all_gather(tag_factors, 'item', axis=1, tiled=True)]
    all_to_all x0 -> x1, starting transfers between devices: none -> 10.1 us  [body(): lax.all_to_all(jnp.stack([user_factors] * lax.axis_size('item')), 'item',...]
    another operation x6 -> x7, local copies, waits for them, and re-layouts: 3.9 us -> 6.71 us
  transfers between devices with their start and end apart: 3 -> 3, of which waited for: 3 -> 2; matrix products, arithmetic and copies ran while one was open for 3% -> 3% of each run, Pallas kernels for 0% -> 0%
where the time goes in v1:
time: 279 us; the launch traced here: 278 us
  waiting for transfers between devices  166 us (59%)
  other arithmetic  60.9 us (22%)
  matrix products  16 us (6%)
  between operations  14.9 us (5%)
  local copies, waits for them, and re-layouts  10.1 us (4%)
  starting transfers between devices  10.1 us (4%)
    psum x1, waiting for transfers between devices, body(): summed_rhs = lax.psum(local_rhs, 'band')  93 us
    all_gather x1, waiting for transfers between devices, body(): tags = lax.all_gather(tag_factors, 'item', axis=1, tiled=True)  72.7 us
    another operation x6, other arithmetic, finish_gram(): jnp.linalg.cholesky(summed_gram + REG * jnp.eye(rank, dtype=jnp.float32))  34.1 us
    another operation x3, other arithmetic, solve_rows(): lax.linalg.triangular_solve(factor, rhs, left_side=False, lower=True, tra...  19.7 us
    dot_general x4, matrix products, inner(): lax.dot_general(left, right, (((0,), (0,)), ((), ())), preferred_element_...  13.1 us
    all_to_all x1, starting transfers between devices, body(): lax.all_to_all(jnp.stack([user_factors] * lax.axis_size('item')), 'item',...  10.1 us
  transfers between devices with their start and end apart: 3, of which 2 were waited for; matrix products, arithmetic and copies ran while one was open for 3% of the time, Pallas kernels for 0%

profile of v1, /device:TPU:32, one launch (start us, length us, event | category | flops | bytes accessed | tf_op | source)
XLA Modules:
  0.0 278.4 jit_solution(17850497471540108323)
XLA Ops:
  6.5 2.9 %stack.2 = bf16[32,6144,8]{1,2,0:T(8,128)(2,1)} broadcast(bf16[6144,8]{0,1:T(8,128)(2,1)} %param.10), dimensions={1,2} | broadcast | bytes 3244032 | tf_op jit(solution)/shard_map/stack | solution.py:38
  9.4 0.0 copy-start.7
  9.4 0.0 copy-start.6
  9.4 0.0 copy-start.3
  9.4 10.1 %all-to-all-start = ((bf16[32,6144,8]{1,2,0:T(8,128)(2,1)}), bf16[32,6144,8]{1,2,0:T(8,128)(2,1)}, u32[]{:S(2)}, u32[]{:S(2)}) async-start(bf16[32,6144,8]{1,2,0:T(8,128)(2,1)} %stack.2), calls=%async_computation | async-start | bytes 6291456 | tf_op jit(solution)/shard_map/all_to_all | solution.py:38
  19.5 0.0 all-gather.2.cloned.1.call-start
  19.5 0.7 all-gather.2.cloned.1.call-update
  20.2 0.0 all-reduce.4.cloned.1.call-start
  20.3 0.0 copy-done.7
  20.3 0.0 copy-done.6
  20.3 0.0 copy-done.3
  20.3 0.0 copy-start
  20.4 1.8 bitcast_multiply_fusion.1
  22.2 2.1 copy-done
  24.3 0.0 copy-start.4
  24.3 3.1 %bitcast_multiply_fusion = bf16[6144,512]{1,0:T(8,128)(2,1)} fusion(bf16[6144,512]{1,0:T(8,128)(2,1)S(1)} %copy-done, bf16[48,512]{1,0:T(8,128)(2,1)S(1)} %convert_element_type.7), kind=kLoop, calls=%fused_computation.2 | loop fusion | flops 3145728 | bytes 12632064 | tf_op jit(solution)/shard_map/mul | solution.py:13
  27.4 72.7 %all-gather.2.cloned.1.call-done = bf16[3072,256]{0,1:T(8,128)(2,1)} async-done(((bf16[3072,8]{0,1:T(8,128)(2,1)}), bf16[3072,256]{0,1:T(8,128)(2,1)}) %all-gather.2.cloned.1.call-update) | async-done | bytes 1572880 | tf_op jit(solution)/shard_map/all_gather | solution.py:40
  100.1 0.0 copy-done.4
  100.1 3.2 %convolution_multiply_fusion = f32[512,256]{1,0:T(8,128)} fusion(bf16[3072,512]{1,0:T(8,128)(2,1)S(1)} %copy-done.4, bf16[3072,256]{0,1:T(8,128)(2,1)} %all-gather.2.cloned.1.call-done), kind=kOutput, calls=%fused_computation.8 | convolution fusion | flops 805437440 | bytes 5242880 | tf_op jit(solution)/shard_map/dot_general | solution.py:18
  103.3 0.0 copy-start.2
  103.3 0.0 all-to-all-done
  103.3 0.0 copy-start.1
  103.3 4.0 %fusion = f32[256,256]{1,0:T(8,128)S(1)} fusion(bf16[32,6144,8]{1,2,0:T(8,128)(2,1)} %all-to-all-done), kind=kOutput, calls=%fused_computation.3 | convolution fusion | flops 805306368 | bytes 3407872 | tf_op jit(solution)/shard_map/dot_general | solution.py:18
  107.3 0.0 copy-done.2
  107.3 0.0 copy-start.8
  107.4 1.3 fusion.7
  108.7 0.0 copy-done.1
  108.7 0.0 copy-done.8
  108.7 4.5 %fusion.4 = f32[512,256]{1,0:T(8,128)} fusion(f32[512,256]{1,0:T(8,128)S(1)} %copy-done.8, bf16[6144,512]{1,0:T(8,128)(2,1)S(1)} %copy-done.1, bf16[32,6144,8]{1,2,0:T(8,128)(2,1)} %all-to-all-done), kind=kOutput, calls=%fused_computation.9 | convolution fusion | flops 1610743808 | bytes 10485760 | tf_op jit(solution)/shard_map/dot_general | solution.py:18
  113.2 0.0 all-reduce.4.cloned.1.call-update
  113.3 93.0 %all-reduce.4.cloned.1.call-done = (f32[512,256]{1,0:T(8,128)}, f32[256,256]{1,0:T(8,128)}) async-done(((f32[512,256]{1,0:T(8,128)}, f32[256,256]{1,0:T(8,128)}), (f32[512,256]{1,0:T(8,128)}, f32[256,256]{1,0:T(8,128)})) %all-reduce.4.cloned.1.call-update) | async-done | bytes 786448 | tf_op jit(solution)/shard_map/psum | solution.py:47
  206.3 0.0 copy-start.5
  206.3 1.0 select_add_fusion
  207.3 0.1 copy.10
  207.5 1.0 fusion.10
  208.5 11.7 %cholesky.49 = f32[128,128]{1,0:T(8,128)S(1)} custom-call(f32[128,128]{1,0:T(8,128)S(1)} %cholesky.115), custom_call_target="Cholesky" | custom-call | tf_op jit(solution)/shard_map/jit(cholesky)/cholesky | solution.py:33
  220.2 9.8 %custom-call.16 = f32[1,128,128]{1,2,0:T(8,128)S(1)} custom-call(f32[1,128,128]{2,1,0:T(8,128)S(1)} %get-tuple-element.28), custom_call_target="InvertDiagBlocksLowerTriangular" | custom-call | tf_op jit(solution)/shard_map/jit(cholesky)/cholesky | solution.py:33
  230.1 0.2 constant_dynamic-update-slice_fusion.1
  230.3 0.3 convolution_subtract_fusion.2
  230.6 11.9 %cholesky.103 = f32[128,128]{1,0:T(8,128)S(1)} custom-call(f32[128,128]{1,0:T(8,128)S(1)} %convolution_subtract_fusion.2), custom_call_target="Cholesky" | custom-call | tf_op jit(solution)/shard_map/jit(cholesky)/cholesky | solution.py:33
  242.5 0.7 compare_reduce_fusion
  244.4 0.1 triangular_solve.70
  244.5 3.8 %while.1 = (s32[]{:T(128)}, f32[256,256]{1,0:T(8,128)S(1)}, s32[2,2]{1,0:T(2,128)S(1)}, f32[2,128,128]{2,1,0:T(8,128)S(1)}, s32[]{:T(128)}) while((s32[]{:T(128)}, f32[256,256]{1,0:T(8,128)S(1)}, s32[2,2]{1,0:T(2,128)S(1)}, f32[2,128,128]{2,1,0:T(8,128)S(1)}, s32[]{:T(128)}) %tuple.23), condition=%wide.while_cond, body=%wide.while_body.sunk | while | flops 2 | bytes 131189 | solution.py:24
  244.5 0.6 fusion.33
  245.1 1.3 bitcast_dynamic-update-slice_fusion.2
  246.4 0.6 fusion.33
  247.0 1.3 bitcast_dynamic-update-slice_fusion.2
  248.3 19.7 %custom-call.17 = f32[2,128,128]{1,2,0:T(8,128)S(1)} custom-call(f32[2,128,128]{2,1,0:T(8,128)S(1)} %get-tuple-element.12), custom_call_target="InvertDiagBlocksLowerTriangular" | custom-call | tf_op jit(solution)/shard_map/triangular_solve | solution.py:24
  268.0 0.0 copy-done.5
  268.0 0.4 fusion.8
  268.4 0.4 convolution_subtract_fusion.1
  268.8 0.4 fusion.16
  269.1 0.4 fusion.15
  269.5 0.6 convolution_subtract_fusion
  270.1 0.4 fusion.14
  270.6 1.0 copy.11
  (12 shorter events, 0.2 us)
Async XLA Ops:
  9.4 10.9 %copy-start.7 = (s32[24,512]{1,0:T(8,128)S(1)}, s32[24,512]{1,0:T(8,128)}, u32[]{:S(2)}) copy-start(s32[24,512]{1,0:T(8,128)} %param.9) | copy-start | bytes 147460
  9.4 10.9 %copy-start.6 = (s32[48,512]{1,0:T(8,128)S(1)}, s32[48,512]{1,0:T(8,128)}, u32[]{:S(2)}) copy-start(s32[48,512]{1,0:T(8,128)} %param.7) | copy-start | bytes 294916
  9.4 10.9 %copy-start.3 = (bf16[3072,512]{1,0:T(8,128)(2,1)S(1)}, bf16[3072,512]{1,0:T(8,128)(2,1)}, u32[]{:S(2)}) copy-start(bf16[3072,512]{1,0:T(8,128)(2,1)} %param.8) | copy-start | bytes 9437188
  9.4 93.9 %all-to-all-start = ((bf16[32,6144,8]{1,2,0:T(8,128)(2,1)}), bf16[32,6144,8]{1,2,0:T(8,128)(2,1)}, u32[]{:S(2)}, u32[]{:S(2)}) async-start(bf16[32,6144,8]{1,2,0:T(8,128)(2,1)} %stack.2), calls=%async_computation | async-start | bytes 6291456 | tf_op jit(solution)/shard_map/all_to_all | solution.py:38
  19.5 80.6 %all-gather.2.cloned.1.call-start = ((), (), s32[]{:S(2)}) async-start(), calls=%async_computation.1 | async-start | bytes 1622016 | tf_op jit(solution)/shard_map/all_gather | solution.py:40
  20.2 186.1 %all-reduce.4.cloned.1.call-start = ((), (), s32[]{:S(2)}) async-start(), calls=%async_computation.2 | async-start | bytes 1572864 | tf_op jit(solution)/shard_map/psum | solution.py:47
  20.3 3.9 %copy-start = (bf16[6144,512]{1,0:T(8,128)(2,1)S(1)}, bf16[6144,512]{1,0:T(8,128)(2,1)}, u32[]{:S(2)}) copy-start(bf16[6144,512]{1,0:T(8,128)(2,1)} %param.6) | copy-start | bytes 18874372
  24.3 75.8 %copy-start.4 = (bf16[3072,512]{1,0:T(8,128)(2,1)S(1)}, bf16[3072,512]{1,0:T(8,128)(2,1)}, u32[]{:S(2)}) copy-start(bf16[3072,512]{1,0:T(8,128)(2,1)} %bitcast_multiply_fusion.1) | copy-start | bytes 9437188
  103.3 4.0 %copy-start.2 = (bf16[3072,256]{0,1:T(8,128)(2,1)S(1)}, bf16[3072,256]{0,1:T(8,128)(2,1)}, u32[]{:S(2)}) copy-start(bf16[3072,256]{0,1:T(8,128)(2,1)} %all-gather.2.cloned.1.call-done) | copy-start | bytes 4718596
  103.3 5.3 %copy-start.1 = (bf16[6144,512]{1,0:T(8,128)(2,1)S(1)}, bf16[6144,512]{1,0:T(8,128)(2,1)}, u32[]{:S(2)}) copy-start(bf16[6144,512]{1,0:T(8,128)(2,1)} %bitcast_multiply_fusion) | copy-start | bytes 18874372
  107.3 1.4 copy-start.8
  206.3 61.7 %copy-start.5 = (f32[512,256]{1,0:T(8,128)S(1)}, f32[512,256]{1,0:T(8,128)}, u32[]{:S(2)}) copy-start(f32[512,256]{1,0:T(8,128)} %get-tuple-element.21) | copy-start | bytes 1572868
Sparse Core Ops, SparseCore 0:
  22.2 77.8 all-gather.1
  113.4 92.8 all-reduce.3
